TPU v7x, 256 devices: a whole 4x4x8 slice. The times are simulated.
256 devices in a mesh: clip: 16 (over z, core), row: 4 (over y), tm: 4 (over x).
Axes of the slice: x: 4, y: 4, z: 8, core: 2. Of those that a mesh axis runs over, the one named last changes fastest.
Arguments:
- frames: bfloat16 [128, 3, 16, 1024], P('clip', None, 'tm', 'row'), may hold values from -6 to 6
- keep_list: int32 [128], P('clip'), may hold values from -1 to 63, as said below
- train_slot: int32 [64], replicated, may hold values from 0 to 63, as said below
- stem_weight: bfloat16 [81, 128], replicated, may hold values from -0.625 to 0.625
- stem_gain: float32 [128], replicated, may hold values from 0.1 to 1.9
- stem_shift: float32 [128], replicated, may hold values from -3 to 3
- mixer_weight: bfloat16 [3, 3, 384, 256], replicated, may hold values from -0.109375 to 0.109375
- mixer_gain: float32 [256], replicated, may hold values from 0.1 to 1.9
- mixer_shift: float32 [256], replicated, may hold values from -3 to 3
- down_weight: bfloat16 [1024, 256], replicated, may hold values from -0.1875 to 0.1875
- down_bias: float32 [256], replicated, may hold values from -3 to 3
Outputs:
- latents: bfloat16 [64, 8, 8, 32, 256], P('clip', 'tm', 'row')
Inputs may be any that keep to these rules, and one draw needn't show every extreme that they name: `keep_list`: each encoder position 0 to 63 is named by exactly one slot, and -1 marks a dropped slot; encoder position e belongs to index e // 4 of clip. `train_slot`: A permutation; training position t belongs to index t // 4 of clip; at most 1 encoder positions of one index of clip go to one index of clip.
All inputs are finite; a program needn't handle non-finite values.
Results may differ from a plain program's by a relative error of at most 0.0053.
Values may be sent and summed in bfloat16 or wider, within the bound.
No kernel may reach another device: no remote copies, remote signals or barrier semaphores. Data moves between devices by JAX's collectives and lax.ppermute only.
A program may use at most 64 MiB of HBM per device.

v0:
```python
import jax
import jax.numpy as jnp
from jax import lax
from jax.sharding import PartitionSpec as P

GROUPS = 32
COLS = 64
eps = 1e-06


def from_behind(shard, axis, by):
    size = lax.axis_size(axis)
    pairs = [(i, i + by) for i in range(size) if 0 <= i + by < size]
    return lax.ppermute(shard, axis, pairs)


def extended_2(cells, sides, width):
    for axis, dim in sides:
        count = lax.axis_size(axis)
        ends = count - 1
        head = lax.slice_in_dim(cells, 0, width, axis=dim)
        tail = lax.slice_in_dim(cells, cells.shape[dim] - width, cells.shape[dim], axis=dim)
        cells = jnp.concatenate(
            [
                lax.ppermute(tail, axis, [(i, (i + 1) % count) for i in range(ends)]),
                cells,
                lax.ppermute(head, axis, [((i + 1) % count, i) for i in range(ends)]),
            ],
            axis=dim,
        )
    return cells


def surround_time(volume):
    frame_n = volume.shape[1]
    earlier = from_behind(volume[:, frame_n - 2 :], "tm", 1)
    opening = jnp.broadcast_to(volume[:, :1], earlier.shape)
    earlier = jnp.where(lax.axis_index("tm") == 0, opening, earlier)
    extended = jnp.concatenate([earlier, volume], axis=1)
    extended = extended_2(extended, (("row", 2),), 1)
    return jnp.pad(extended, ((0, 0), (0, 0), (0, 0), (1, 1), (0, 0)))


def norm_silu(hidden, gain, shift):
    batch_n, cell_n, chan_n = hidden.shape
    per_group = chan_n // GROUPS
    value_sum = jnp.sum(hidden, axis=1).reshape(batch_n, GROUPS, per_group).sum(-1)
    square_sum = jnp.sum(hidden * hidden, axis=1).reshape(batch_n, GROUPS, per_group).sum(-1)
    value_sum, square_sum = lax.psum((value_sum, square_sum), ("row", "tm"))
    cell_count = cell_n * per_group * lax.axis_size("row") * lax.axis_size("tm")
    group_mean = value_sum / cell_count
    spread = square_sum / cell_count - group_mean * group_mean
    inverse = lax.rsqrt(spread + eps)
    mean_full = jnp.repeat(group_mean, per_group, axis=1)[:, None, :]
    scale_full = jnp.repeat(inverse, per_group, axis=1)[:, None, :] * gain
    return jax.nn.silu((hidden - mean_full) * scale_full + shift)


def encode(clips, params, col_n, surround):
    (
        stem_weight,
        stem_gain,
        stem_shift,
        mixer_weight,
        mixer_gain,
        mixer_shift,
        down_weight,
        down_bias,
    ) = params
    batch_n, chan_in, frame_n, row_cells = clips.shape
    row_n = row_cells // col_n
    cell_n = frame_n * row_n * col_n
    volume = clips.reshape(batch_n, chan_in, frame_n, row_n, col_n).transpose(0, 2, 3, 4, 1)
    padded = surround(volume)
    tap_views = []
    for time_tap in range(3):
        for row_tap in range(3):
            for col_tap in range(3):
                tap_views.append(
                    padded[
                        :,
                        time_tap : time_tap + frame_n,
                        row_tap : row_tap + row_n,
                        col_tap : col_tap + col_n,
                    ]
                )
    patches = jnp.concatenate(tap_views, axis=-1).reshape(batch_n * cell_n, 27 * chan_in)
    stem = jnp.dot(patches, stem_weight, preferred_element_type=jnp.float32).reshape(
        batch_n, cell_n, -1
    )
    hidden = norm_silu(stem, stem_gain, stem_shift).astype(jnp.bfloat16)
    padded = surround(hidden.reshape(batch_n, frame_n, row_n, col_n, -1))
    accumulated = jnp.zeros((batch_n * cell_n, mixer_weight.shape[3]), jnp.float32)
    for time_tap in range(3):
        for row_tap in range(3):
            tap_strip = jnp.concatenate(
                [
                    padded[
                        :,
                        time_tap : time_tap + frame_n,
                        row_tap : row_tap + row_n,
                        col_tap : col_tap + col_n,
                    ]
                    for col_tap in range(3)
                ],
                axis=-1,
            )
            accumulated = accumulated + jnp.dot(
                tap_strip.reshape(-1, tap_strip.shape[-1]),
                mixer_weight[time_tap, row_tap],
                preferred_element_type=jnp.float32,
            )
    activated = norm_silu(accumulated.reshape(batch_n, cell_n, -1), mixer_gain, mixer_shift).astype(
        jnp.bfloat16
    )
    activated = activated.reshape(batch_n, frame_n, row_n, col_n, -1)
    pooled = (
        (activated[:, 0::2].astype(jnp.float32) + activated[:, 1::2].astype(jnp.float32)) * 0.5
    ).astype(jnp.bfloat16)
    chan_out = pooled.shape[-1]
    blocks = (
        pooled.reshape(batch_n, frame_n // 2, row_n // 2, 2, col_n // 2, 2, chan_out)
        .transpose(0, 1, 2, 4, 3, 5, 6)
        .reshape(-1, 4 * chan_out)
    )
    latent = jnp.dot(blocks, down_weight, preferred_element_type=jnp.float32) + down_bias
    return latent.astype(jnp.bfloat16).reshape(
        batch_n, frame_n // 2, row_n // 2, col_n // 2, chan_out
    )


def encode_layout(clips, params):
    return encode(clips, params, COLS, surround_time)


def select_rows(target, items, slot_n):
    flattened = items.reshape(items.shape[0], -1)
    wanted = jnp.arange(slot_n, dtype=jnp.int32)
    picker = (wanted[:, None] == target[None, :]).astype(jnp.bfloat16)
    return jnp.dot(picker, flattened, preferred_element_type=jnp.float32).astype(jnp.bfloat16)


def combine_sources(received):
    return jnp.sum(received.astype(jnp.float32), axis=0).astype(jnp.bfloat16)


def local(
    frames,
    keep_list,
    train_slot,
    stem_weight,
    stem_gain,
    stem_shift,
    mixer_weight,
    mixer_gain,
    mixer_shift,
    down_weight,
    down_bias,
):
    params = (
        stem_weight,
        stem_gain,
        stem_shift,
        mixer_weight,
        mixer_gain,
        mixer_shift,
        down_weight,
        down_bias,
    )
    group_n = lax.axis_size("clip")
    enc_dev = train_slot.shape[0] // group_n
    slot_n = group_n * enc_dev
    safe_keep = jnp.maximum(keep_list, 0)
    composed = jnp.where(keep_list >= 0, train_slot[safe_keep], -1)
    packed = select_rows(composed, frames, slot_n).reshape((group_n, enc_dev) + frames.shape[1:])
    received = lax.all_to_all(packed, "clip", split_axis=0, concat_axis=0, tiled=True)
    return encode_layout(combine_sources(received), params)


def solution(mesh):
    return jax.shard_map(
        local,
        mesh=mesh,
        in_specs=(
            P("clip", None, "tm", "row"),
            P("clip"),
            P(),
            P(),
            P(),
            P(),
            P(),
            P(),
            P(),
            P(),
            P(),
        ),
        out_specs=P("clip", "tm", "row", None, None),
        check_vma=False,
    )
```

profile of v0, /device:TPU:32, one launch (start us, length us, event | category | flops | bytes accessed | tf_op | source)
XLA Modules:
  0.0 240.4 jit_solution(16834706322915642902)
XLA Ops:
  1.6 1.3 gather_fusion
  4.8 8.6 %all-to-all-start = ((bf16[16,4,3,4,256]{4,3,2,1,0:T(4,128)(2,1)}), bf16[16,4,3,4,256]{4,3,2,1,0:T(4,128)(2,1)S(1)}, u32[]{:S(2)}, u32[]{:S(2)}) async-start(bf16[16,4,3,4,256]{4,3,2,1,0:T(4,128)(2,1)} %reshape.120), calls=%async_computation | async-start | bytes 786432 | tf_op jit(solution)/shard_map/all_to_all | solution.py:176
  13.4 11.9 %all-to-all-done = bf16[16,4,3,4,256]{4,3,2,1,0:T(4,128)(2,1)S(1)} async-done(((bf16[16,4,3,4,256]{4,3,2,1,0:T(4,128)(2,1)}), bf16[16,4,3,4,256]{4,3,2,1,0:T(4,128)(2,1)S(1)}, u32[]{:S(2)}, u32[]{:S(2)}) %all-to-all-start) | async-done | bytes 393248 | tf_op jit(solution)/shard_map/all_to_all | solution.py:176
  25.6 3.4 %collective-permute-start = (bf16[4,2,4,64,3]{3,2,4,1,0:T(4,128)(2,1)S(1)}, bf16[4,2,4,64,3]{3,2,4,1,0:T(4,128)(2,1)S(1)}, u32[]{:S(2)}, u32[]{:S(2)}) collective-permute-start(bf16[4,2,4,64,3]{3,2,4,1,0:T(4,128)(2,1)S(1)} %slice.325), channel_id=1, source_target_pairs={{0,1},{1,2},{2,3},{4,5},{5,6},{6,7},{8,9},{9,10},{10,11},{12,13},{... | collective-permute-start | bytes 36872 | tf_op jit(solution)/shard_map/ppermute | solution.py:14
  29.0 1.5 collective-permute-done
  32.0 4.5 %collective-permute-start.1 = (bf16[4,6,1,64,3]{3,2,4,1,0:T(2,128)(2,1)S(1)}, bf16[4,6,1,64,3]{3,2,4,1,0:T(2,128)(2,1)S(1)}, u32[]{:S(2)}, u32[]{:S(2)}) collective-permute-start(bf16[4,6,1,64,3]{3,2,4,1,0:T(2,128)(2,1)S(1)} %get-tuple-element.43), channel_id=1, source_target_pairs={{0,4},{4,8},{8,12},{1,5},{5,9},{9,13},{2,6},{6,10},{10,14},{3,7},{... | collective-permute-start | bytes 27656 | tf_op jit(solution)/shard_map/ppermute | solution.py:25
  36.5 1.6 collective-permute-done.1
  40.5 2.1 copy.36
  42.7 1.7 fusion.49
  44.7 42.5 %all-reduce.3 = (f32[4,32]{1,0:T(4,128)S(1)}, f32[4,32]{1,0:T(4,128)S(1)}) all-reduce(f32[4,32]{1,0:T(4,128)S(1)} %reduce_sum.88, f32[4,32]{1,0:T(4,128)S(1)} %reduce_sum.86), channel_id=1, replica_groups=mesh['clip'=16,'row'=4,'tm'=4] {'row','tm'}, use_global_device_ids=true, to_apply=%region_6.7 | all-reduce | flops 256 | bytes 2048 | tf_op jit(solution)/shard_map/psum | solution.py:49
  88.4 1.3 collective-permute-start.3
  89.7 6.6 %collective-permute-done.3 = bf16[4,2,4,64,128]{4,3,2,1,0:T(8,128)(2,1)S(1)} collective-permute-done((bf16[4,2,4,64,128]{4,3,2,1,0:T(8,128)(2,1)S(1)}, bf16[4,2,4,64,128]{4,3,2,1,0:T(8,128)(2,1)S(1)}, u32[]{:S(2)}, u32[]{:S(2)}) %collective-permute-start.3) | collective-permute-done | bytes 524320 | tf_op jit(solution)/shard_map/ppermute | solution.py:14
  97.8 4.8 %collective-permute-start.4 = (bf16[4,6,1,64,128]{4,3,2,1,0:T(8,128)(2,1)S(1)}, bf16[4,6,1,64,128]{4,3,2,1,0:T(8,128)(2,1)S(1)}, u32[]{:S(2)}, u32[]{:S(2)}) collective-permute-start(bf16[4,6,1,64,128]{4,3,2,1,0:T(8,128)(2,1)S(1)} %get-tuple-element.39), channel_id=1, source_target_pairs={{0,4},{4,8},{8,12},{1,5},{5,9},{9,13},{2,6},{6,10},{10,14},{3,7},{... | collective-permute-start | bytes 1179656 | tf_op jit(solution)/shard_map/ppermute | solution.py:25
  103.6 2.6 %collective-permute-done.5 = bf16[4,6,1,64,128]{4,3,2,1,0:T(8,128)(2,1)S(1)} collective-permute-done((bf16[4,6,1,64,128]{4,3,2,1,0:T(8,128)(2,1)S(1)}, bf16[4,6,1,64,128]{4,3,2,1,0:T(8,128)(2,1)S(1)}, u32[]{:S(2)}, u32[]{:S(2)}) %collective-permute-start.5) | collective-permute-done | bytes 393248 | tf_op jit(solution)/shard_map/ppermute | solution.py:27
  106.2 1.5 collective-permute-done.4
  107.6 1.4 select_maximum_fusion
  109.1 6.2 %fusion.50 = (bf16[4,4,4,64,128]{4,3,2,1,0:T(8,128)(2,1)}, bf16[4,4,4,64,128]{4,3,2,1,0:T(8,128)(2,1)}, bf16[4,4,4,64,128]{4,3,2,1,0:T(8,128)(2,1)}, bf16[4,4,4,...) fusion(bf16[4,6,6,66,128]{4,3,2,1,0:T(8,128)(2,1)S(1)} %select_, ...), kind=kLoop, calls=%fused_computation.143 | loop fusion | bytes 37748736 | tf_op jit(solution)/shard_map/slice | solution.py:98
  128.2 1.3 pad_maximum_fusion.5
  135.2 3.2 %bitcast_reduce_fusion = (f32[4,256]{1,0:T(4,128)S(1)}, f32[4,256]{1,0:T(4,128)S(1)}, f32[4096,256]{1,0:T(8,128)}) fusion(f32[4096,256]{1,0:T(8,128)S(1)} %convolution_add_fusion.1, bf16[4096,384]{1,0:T(8,128)(2,1)S(1)} %bitcast.87, bf16[3,3,384,256]{3,2,1,0:T(8,128)(2,1)S(1)} %copy-done.8), kind=kOutput, calls=%fused_computation.14 | convolution fusion | flops 809498624 | bytes 11739136 | tf_op jit(solution)/shard_map/dot_general | solution.py:108
  138.8 38.2 %all-reduce.2 = (f32[4,32]{1,0:T(4,128)S(1)}, f32[4,32]{1,0:T(4,128)S(1)}) all-reduce(f32[4,32]{1,0:T(4,128)S(1)} %reduce_sum.92, f32[4,32]{1,0:T(4,128)S(1)} %reduce_sum.90), channel_id=1, replica_groups=mesh['clip'=16,'row'=4,'tm'=4] {'row','tm'}, use_global_device_ids=true, to_apply=%region_12.13 | all-reduce | flops 256 | bytes 2048 | tf_op jit(solution)/shard_map/psum | solution.py:49
  177.4 6.2 %fusion.4 = bf16[4,4,4,64,256]{4,1,3,2,0:T(4,128)(2,1)S(1)} fusion(f32[4,4,4,64,256]{4,3,2,1,0:T(8,128)} %bitcast.86, f32[256]{0:T(256)S(1)} %copy-done.13, f32[4,256]{1,0:T(4,128)S(1)} %broadcast_multiply_fusion, f32[4,256]{1,0:T(4,128)S(1)} %sub.31), kind=kLoop, calls=%fused_computation.19 | loop fusion | flops 8388608 | bytes 6300672 | tf_op jit(solution)/shard_map/convert_element_type | solution.py:113
  183.6 25.5 %slice.321 = bf16[4,2,4,64,256]{4,1,3,2,0:T(2,128)(2,1)} slice(bf16[4,4,4,64,256]{4,1,3,2,0:T(4,128)(2,1)S(1)} %fusion.4), slice={[0:4:1], [1:4:2], [0:4:1], [0:64:1], [0:256:1]} | slice | bytes 2097152 | tf_op jit(solution)/shard_map/slice | solution.py:118
  209.1 25.4 %slice.320 = bf16[4,2,4,64,256]{4,1,3,2,0:T(2,128)(2,1)} slice(bf16[4,4,4,64,256]{4,1,3,2,0:T(4,128)(2,1)S(1)} %fusion.4), slice={[0:4:1], [0:4:2], [0:4:1], [0:64:1], [0:256:1]} | slice | bytes 2097152 | tf_op jit(solution)/shard_map/slice | solution.py:118
  234.5 3.1 %multiply_convert_fusion = bf16[4,2,4,64,256]{4,1,3,2,0:T(2,128)(2,1)S(1)} fusion(bf16[4,2,4,64,256]{4,1,3,2,0:T(2,128)(2,1)} %slice.321, bf16[4,2,4,64,256]{4,1,3,2,0:T(2,128)(2,1)} %slice.320), kind=kLoop, calls=%fused_computation.44 | loop fusion | flops 2621440 | bytes 3145728 | tf_op jit(solution)/shard_map/convert_element_type | solution.py:119
  (123 shorter events, 33.3 us)
Async XLA Ops:
  0.0 239.3 %copy-start = (bf16[1024,256]{1,0:T(8,128)(2,1)S(1)}, bf16[1024,256]{1,0:T(8,128)(2,1)}, u32[]{:S(2)}) copy-start(bf16[1024,256]{1,0:T(8,128)(2,1)} %param.20) | copy-start | bytes 1572868
  4.8 20.5 %all-to-all-start = ((bf16[16,4,3,4,256]{4,3,2,1,0:T(4,128)(2,1)}), bf16[16,4,3,4,256]{4,3,2,1,0:T(4,128)(2,1)S(1)}, u32[]{:S(2)}, u32[]{:S(2)}) async-start(bf16[16,4,3,4,256]{4,3,2,1,0:T(4,128)(2,1)} %reshape.120), calls=%async_computation | async-start | bytes 786432 | tf_op jit(solution)/shard_map/all_to_all | solution.py:176
  25.5 17.2 %copy-start.11 = (bf16[81,128]{1,0:T(8,128)(2,1)S(1)}, bf16[81,128]{1,0:T(8,128)(2,1)}, u32[]{:S(2)}) copy-start(bf16[81,128]{1,0:T(8,128)(2,1)} %param.14) | copy-start | bytes 62212
  25.6 4.9 %collective-permute-start = (bf16[4,2,4,64,3]{3,2,4,1,0:T(4,128)(2,1)S(1)}, bf16[4,2,4,64,3]{3,2,4,1,0:T(4,128)(2,1)S(1)}, u32[]{:S(2)}, u32[]{:S(2)}) collective-permute-start(bf16[4,2,4,64,3]{3,2,4,1,0:T(4,128)(2,1)S(1)} %slice.325), channel_id=1, source_target_pairs={{0,1},{1,2},{2,3},{4,5},{5,6},{6,7},{8,9},{9,10},{10,11},{12,13},{... | collective-permute-start | bytes 36872 | tf_op jit(solution)/shard_map/ppermute | solution.py:14
  30.7 5.9 %collective-permute-start.2 = (bf16[4,6,1,64,3]{3,2,4,1,0:T(2,128)(2,1)S(1)}, bf16[4,6,1,64,3]{3,2,4,1,0:T(2,128)(2,1)S(1)}, u32[]{:S(2)}, u32[]{:S(2)}) collective-permute-start(bf16[4,6,1,64,3]{3,2,4,1,0:T(2,128)(2,1)S(1)} %get-tuple-element.44), channel_id=1, source_target_pairs={{4,0},{8,4},{12,8},{5,1},{9,5},{13,9},{6,2},{10,6},{14,10},{7,3},{... | collective-permute-start | bytes 27656 | tf_op jit(solution)/shard_map/ppermute | solution.py:27
  32.0 6.2 %collective-permute-start.1 = (bf16[4,6,1,64,3]{3,2,4,1,0:T(2,128)(2,1)S(1)}, bf16[4,6,1,64,3]{3,2,4,1,0:T(2,128)(2,1)S(1)}, u32[]{:S(2)}, u32[]{:S(2)}) collective-permute-start(bf16[4,6,1,64,3]{3,2,4,1,0:T(2,128)(2,1)S(1)} %get-tuple-element.43), channel_id=1, source_target_pairs={{0,4},{4,8},{8,12},{1,5},{5,9},{9,13},{2,6},{6,10},{10,14},{3,7},{... | collective-permute-start | bytes 27656 | tf_op jit(solution)/shard_map/ppermute | solution.py:25
  40.3 47.4 %copy-start.14 = (f32[128]{0:T(128)S(1)}, f32[128]{0:T(128)}, u32[]{:S(2)}) copy-start(f32[128]{0:T(128)} %param.15) | copy-start | bytes 1540
  40.3 47.4 %copy-start.15 = (f32[128]{0:T(128)S(1)}, f32[128]{0:T(128)}, u32[]{:S(2)}) copy-start(f32[128]{0:T(128)} %param.16) | copy-start | bytes 1540
  88.4 8.0 %collective-permute-start.3 = (bf16[4,2,4,64,128]{4,3,2,1,0:T(8,128)(2,1)S(1)}, bf16[4,2,4,64,128]{4,3,2,1,0:T(8,128)(2,1)S(1)}, u32[]{:S(2)}, u32[]{:S(2)}) collective-permute-start(bf16[4,2,4,64,128]{4,3,2,1,0:T(8,128)(2,1)S(1)} %slice.357), channel_id=1, source_target_pairs={{0,1},{1,2},{2,3},{4,5},{5,6},{6,7},{8,9},{9,10},{10,11},{12,13},{... | collective-permute-start | bytes 1572872 | tf_op jit(solution)/shard_map/ppermute | solution.py:14
  96.5 9.7 %collective-permute-start.5 = (bf16[4,6,1,64,128]{4,3,2,1,0:T(8,128)(2,1)S(1)}, bf16[4,6,1,64,128]{4,3,2,1,0:T(8,128)(2,1)S(1)}, u32[]{:S(2)}, u32[]{:S(2)}) collective-permute-start(bf16[4,6,1,64,128]{4,3,2,1,0:T(8,128)(2,1)S(1)} %get-tuple-element.40), channel_id=1, source_target_pairs={{4,0},{8,4},{12,8},{5,1},{9,5},{13,9},{6,2},{10,6},{14,10},{7,3},{... | collective-permute-start | bytes 1179656 | tf_op jit(solution)/shard_map/ppermute | solution.py:27
  97.8 9.8 %collective-permute-start.4 = (bf16[4,6,1,64,128]{4,3,2,1,0:T(8,128)(2,1)S(1)}, bf16[4,6,1,64,128]{4,3,2,1,0:T(8,128)(2,1)S(1)}, u32[]{:S(2)}, u32[]{:S(2)}) collective-permute-start(bf16[4,6,1,64,128]{4,3,2,1,0:T(8,128)(2,1)S(1)} %get-tuple-element.39), channel_id=1, source_target_pairs={{0,4},{4,8},{8,12},{1,5},{5,9},{9,13},{2,6},{6,10},{10,14},{3,7},{... | collective-permute-start | bytes 1179656 | tf_op jit(solution)/shard_map/ppermute | solution.py:25
  116.7 1.2 copy-start.1
  116.7 1.5 copy-start.2
  116.7 1.8 copy-start.3
  118.6 1.5 copy-start.8
  124.9 1.3 copy-start.6
  124.9 1.5 copy-start.7
  130.8 1.3 copy-start.4
  130.8 1.5 copy-start.5
  132.4 1.2 copy-start.9
  132.4 1.5 copy-start.10
  135.2 42.1 %copy-start.12 = (f32[256]{0:T(256)S(1)}, f32[256]{0:T(256)}, u32[]{:S(2)}) copy-start(f32[256]{0:T(256)} %param.18) | copy-start | bytes 3076
  135.2 42.2 %copy-start.13 = (f32[256]{0:T(256)S(1)}, f32[256]{0:T(256)}, u32[]{:S(2)}) copy-start(f32[256]{0:T(256)} %param.19) | copy-start | bytes 3076
  234.5 4.8 %copy-start.16 = (f32[256]{0:T(256)S(1)}, f32[256]{0:T(256)}, u32[]{:S(2)}) copy-start(f32[256]{0:T(256)} %param.21) | copy-start | bytes 3076
where the time goes:
time: 241 us; the launch traced here: 240 us
  blocking collectives  80.7 us (33%)
  local copies, waits for them, and re-layouts  71.9 us (30%)
  waiting for transfers between devices  25.7 us (11%)
  starting transfers between devices  25.2 us (10%)
  other arithmetic  20.1 us (8%)
  matrix products  16.2 us (7%)
    psum x2, blocking collectives, norm_silu(): value_sum, square_sum = lax.psum((value_sum, square_sum), ('row', 'tm'))  80.7 us
    slice x1, local copies, waits for them, and re-layouts, encode(): activated[:, 1::2].astype(jnp.float32)  25.5 us
    slice x1, local copies, waits for them, and re-layouts, encode(): activated[:, 0::2].astype(jnp.float32)  25.4 us
    dot_general x9, matrix products, encode(): jnp.dot(tap_strip.reshape(-1, tap_strip.shape[-1]), mixer_weight[time_tap...  13.2 us
    all_to_all x1, waiting for transfers between devices, local(): lax.all_to_all(packed, 'clip', split_axis=0, concat_axis=0, tiled=True)  11.9 us
    ppermute x2, starting transfers between devices, extended_2(): lax.ppermute(tail, axis, [(i, (i + 1) % count) for i in range(ends)])  9.3 us
    all_to_all x1, starting transfers between devices, local(): lax.all_to_all(packed, 'clip', split_axis=0, concat_axis=0, tiled=True)  8.59 us
    slice x3, local copies, waits for them, and re-layouts, encode(): padded[:, time_tap:time_tap + frame_n, row_tap:row_tap + row_n, col_tap:c...  8.15 us
  transfers between devices with their start and end apart: 7, of which 6 were waited for; matrix products, arithmetic and copies ran while one was open for 0% of the time, Pallas kernels for 0%

commit v1 on v0

--- a/solution.py
+++ b/solution.py
@@ -46,7 +46,7 @@
     per_group = chan_n // GROUPS
     value_sum = jnp.sum(hidden, axis=1).reshape(batch_n, GROUPS, per_group).sum(-1)
     square_sum = jnp.sum(hidden * hidden, axis=1).reshape(batch_n, GROUPS, per_group).sum(-1)
-    value_sum, square_sum = lax.psum((value_sum, square_sum), ("row", "tm"))
+    value_sum, square_sum = lax.psum(lax.psum((value_sum, square_sum), "tm"), "row")
     cell_count = cell_n * per_group * lax.axis_size("row") * lax.axis_size("tm")
     group_mean = value_sum / cell_count
     spread = square_sum / cell_count - group_mean * group_mean

time: 241 us -> 205 us (0.85)
  blocking collectives: 80.7 us -> 43.6 us
    psum x2 -> x4, blocking collectives: 80.7 us -> 43.6 us  [the longest x2 22 us: norm_silu(): lax.psum(lax.psum((value_sum, square_sum), 'tm'), 'row')]
  transfers between devices with their start and end apart: 7 -> 7, of which waited for: 6 -> 6; matrix products, arithmetic and copies ran while one was open for 0% -> 1% of each run, Pallas kernels for 0% -> 0%
where the time goes in v1:
time: 205 us; the launch traced here: 204 us
  local copies, waits for them, and re-layouts  71.9 us (35%)
  blocking collectives  43.6 us (21%)
  waiting for transfers between devices  25.7 us (13%)
  starting transfers between devices  25.4 us (12%)
  other arithmetic  20.1 us (10%)
  matrix products  16.2 us (8%)
    slice x1, local copies, waits for them, and re-layouts, encode(): activated[:, 1::2].astype(jnp.float32)  25.5 us
    slice x1, local copies, waits for them, and re-layouts, encode(): activated[:, 0::2].astype(jnp.float32)  25.3 us
    psum x2, blocking collectives, norm_silu(): lax.psum(lax.psum((value_sum, square_sum), 'tm'), 'row')  22 us
    psum x2, blocking collectives, norm_silu(): lax.psum((value_sum, square_sum), 'tm')  21.7 us
    dot_general x9, matrix products, encode(): jnp.dot(tap_strip.reshape(-1, tap_strip.shape[-1]), mixer_weight[time_tap...  13.2 us
    all_to_all x1, waiting for transfers between devices, local(): lax.all_to_all(packed, 'clip', split_axis=0, concat_axis=0, tiled=True)  11.9 us
    ppermute x2, starting transfers between devices, extended_2(): lax.ppermute(tail, axis, [(i, (i + 1) % count) for i in range(ends)])  9.3 us
    all_to_all x1, starting transfers between devices, local(): lax.all_to_all(packed, 'clip', split_axis=0, concat_axis=0, tiled=True)  8.59 us
  transfers between devices with their start and end apart: 7, of which 6 were waited for; matrix products, arithmetic and copies ran while one was open for 1% of the time, Pallas kernels for 0%

profile of v1, /device:TPU:32, one launch (start us, length us, event | category | flops | bytes accessed | tf_op | source)
XLA Modules:
  0.0 203.6 jit_solution(6277316989690004933)
XLA Ops:
  4.8 8.6 %all-to-all-start = ((bf16[16,4,3,4,256]{4,3,2,1,0:T(4,128)(2,1)}), bf16[16,4,3,4,256]{4,3,2,1,0:T(4,128)(2,1)S(1)}, u32[]{:S(2)}, u32[]{:S(2)}) async-start(bf16[16,4,3,4,256]{4,3,2,1,0:T(4,128)(2,1)} %reshape.120), calls=%async_computation | async-start | bytes 786432 | tf_op jit(solution)/shard_map/all_to_all | solution.py:176
  13.4 11.9 %all-to-all-done = bf16[16,4,3,4,256]{4,3,2,1,0:T(4,128)(2,1)S(1)} async-done(((bf16[16,4,3,4,256]{4,3,2,1,0:T(4,128)(2,1)}), bf16[16,4,3,4,256]{4,3,2,1,0:T(4,128)(2,1)S(1)}, u32[]{:S(2)}, u32[]{:S(2)}) %all-to-all-start) | async-done | bytes 393248 | tf_op jit(solution)/shard_map/all_to_all | solution.py:176
  25.6 3.4 %collective-permute-start = (bf16[4,2,4,64,3]{3,2,4,1,0:T(4,128)(2,1)S(1)}, bf16[4,2,4,64,3]{3,2,4,1,0:T(4,128)(2,1)S(1)}, u32[]{:S(2)}, u32[]{:S(2)}) collective-permute-start(bf16[4,2,4,64,3]{3,2,4,1,0:T(4,128)(2,1)S(1)} %slice.325), channel_id=1, source_target_pairs={{0,1},{1,2},{2,3},{4,5},{5,6},{6,7},{8,9},{9,10},{10,11},{12,13},{... | collective-permute-start | bytes 36872 | tf_op jit(solution)/shard_map/ppermute | solution.py:14
  29.0 1.5 collective-permute-done
  32.0 4.5 %collective-permute-start.1 = (bf16[4,6,1,64,3]{3,2,4,1,0:T(2,128)(2,1)S(1)}, bf16[4,6,1,64,3]{3,2,4,1,0:T(2,128)(2,1)S(1)}, u32[]{:S(2)}, u32[]{:S(2)}) collective-permute-start(bf16[4,6,1,64,3]{3,2,4,1,0:T(2,128)(2,1)S(1)} %get-tuple-element.47), channel_id=1, source_target_pairs={{0,4},{4,8},{8,12},{1,5},{5,9},{9,13},{2,6},{6,10},{10,14},{3,7},{... | collective-permute-start | bytes 27656 | tf_op jit(solution)/shard_map/ppermute | solution.py:25
  36.5 1.6 collective-permute-done.1
  40.5 2.1 %copy.36 = bf16[4,4,4,64,81]{4,3,2,1,0:T(8,128)(2,1)} copy(bf16[4,4,4,64,81]{3,2,4,1,0:T(4,128)(2,1)S(1)} %constant_dynamic-update-slice_fusion) | data formatting | bytes 1327104 | tf_op jit(solution)/shard_map/concatenate | solution.py:87
  42.7 1.6 fusion.49
  44.7 11.3 %all-reduce.3 = (f32[4,32]{1,0:T(4,128)S(1)}, f32[4,32]{1,0:T(4,128)S(1)}) all-reduce(f32[4,32]{1,0:T(4,128)S(1)} %reduce_sum.88, f32[4,32]{1,0:T(4,128)S(1)} %reduce_sum.86), channel_id=1, replica_groups=mesh['clip'=16,'row'=4,'tm'=4] {'tm'}, use_global_device_ids=true, to_apply=%region_7.8 | all-reduce | flops 256 | bytes 2048 | tf_op jit(solution)/shard_map/psum | solution.py:49
  56.0 11.8 %all-reduce.5 = (f32[4,32]{1,0:T(4,128)S(1)}, f32[4,32]{1,0:T(4,128)S(1)}) all-reduce(f32[4,32]{1,0:T(4,128)S(1)} %get-tuple-element.11, f32[4,32]{1,0:T(4,128)S(1)} %get-tuple-element.12), channel_id=1, replica_groups=mesh['clip'=16,'row'=4,'tm'=4] {'row'}, use_global_device_ids=true, to_apply=%region_8.9 | all-reduce | flops 256 | bytes 2048 | tf_op jit(solution)/shard_map/psum | solution.py:49
  68.9 1.6 collective-permute-start.3
  70.5 6.6 %collective-permute-done.3 = bf16[4,2,4,64,128]{4,3,2,1,0:T(8,128)(2,1)S(1)} collective-permute-done((bf16[4,2,4,64,128]{4,3,2,1,0:T(8,128)(2,1)S(1)}, bf16[4,2,4,64,128]{4,3,2,1,0:T(8,128)(2,1)S(1)}, u32[]{:S(2)}, u32[]{:S(2)}) %collective-permute-start.3) | collective-permute-done | bytes 524320 | tf_op jit(solution)/shard_map/ppermute | solution.py:14
  78.6 4.8 %collective-permute-start.4 = (bf16[4,6,1,64,128]{4,3,2,1,0:T(8,128)(2,1)S(1)}, bf16[4,6,1,64,128]{4,3,2,1,0:T(8,128)(2,1)S(1)}, u32[]{:S(2)}, u32[]{:S(2)}) collective-permute-start(bf16[4,6,1,64,128]{4,3,2,1,0:T(8,128)(2,1)S(1)} %get-tuple-element.43), channel_id=1, source_target_pairs={{0,4},{4,8},{8,12},{1,5},{5,9},{9,13},{2,6},{6,10},{10,14},{3,7},{... | collective-permute-start | bytes 1179656 | tf_op jit(solution)/shard_map/ppermute | solution.py:25
  84.4 2.6 %collective-permute-done.5 = bf16[4,6,1,64,128]{4,3,2,1,0:T(8,128)(2,1)S(1)} collective-permute-done((bf16[4,6,1,64,128]{4,3,2,1,0:T(8,128)(2,1)S(1)}, bf16[4,6,1,64,128]{4,3,2,1,0:T(8,128)(2,1)S(1)}, u32[]{:S(2)}, u32[]{:S(2)}) %collective-permute-start.5) | collective-permute-done | bytes 393248 | tf_op jit(solution)/shard_map/ppermute | solution.py:27
  86.9 1.5 collective-permute-done.4
  88.4 1.4 select_maximum_fusion
  89.8 6.3 %fusion.50 = (bf16[4,4,4,64,128]{4,3,2,1,0:T(8,128)(2,1)}, bf16[4,4,4,64,128]{4,3,2,1,0:T(8,128)(2,1)}, bf16[4,4,4,64,128]{4,3,2,1,0:T(8,128)(2,1)}, bf16[4,4,4,...) fusion(bf16[4,6,6,66,128]{4,3,2,1,0:T(8,128)(2,1)S(1)} %select_, ...), kind=kLoop, calls=%fused_computation.143 | loop fusion | bytes 37748736 | tf_op jit(solution)/shard_map/slice | solution.py:98
  116.0 3.2 %bitcast_reduce_fusion = (f32[4,256]{1,0:T(4,128)S(1)}, f32[4,256]{1,0:T(4,128)S(1)}, f32[4096,256]{1,0:T(8,128)}) fusion(f32[4096,256]{1,0:T(8,128)S(1)} %convolution_add_fusion.1, bf16[4096,384]{1,0:T(8,128)(2,1)S(1)} %bitcast.87, bf16[3,3,384,256]{3,2,1,0:T(8,128)(2,1)S(1)} %copy-done.8), kind=kOutput, calls=%fused_computation.14 | convolution fusion | flops 809498624 | bytes 11739136 | tf_op jit(solution)/shard_map/dot_general | solution.py:108
  119.6 10.3 %all-reduce.2 = (f32[4,32]{1,0:T(4,128)S(1)}, f32[4,32]{1,0:T(4,128)S(1)}) all-reduce(f32[4,32]{1,0:T(4,128)S(1)} %reduce_sum.92, f32[4,32]{1,0:T(4,128)S(1)} %reduce_sum.90), channel_id=1, replica_groups=mesh['clip'=16,'row'=4,'tm'=4] {'tm'}, use_global_device_ids=true, to_apply=%region_15.16 | all-reduce | flops 256 | bytes 2048 | tf_op jit(solution)/shard_map/psum | solution.py:49
  129.9 10.2 %all-reduce.4 = (f32[4,32]{1,0:T(4,128)S(1)}, f32[4,32]{1,0:T(4,128)S(1)}) all-reduce(f32[4,32]{1,0:T(4,128)S(1)} %get-tuple-element.9, f32[4,32]{1,0:T(4,128)S(1)} %get-tuple-element.10), channel_id=1, replica_groups=mesh['clip'=16,'row'=4,'tm'=4] {'row'}, use_global_device_ids=true, to_apply=%region_16.17 | all-reduce | flops 256 | bytes 2048 | tf_op jit(solution)/shard_map/psum | solution.py:49
  140.6 6.2 %fusion.4 = bf16[4,4,4,64,256]{4,1,3,2,0:T(4,128)(2,1)S(1)} fusion(f32[4,4,4,64,256]{4,3,2,1,0:T(8,128)} %bitcast.86, f32[256]{0:T(256)S(1)} %copy-done.13, f32[4,256]{1,0:T(4,128)S(1)} %broadcast_multiply_fusion, f32[4,256]{1,0:T(4,128)S(1)} %sub.31), kind=kLoop, calls=%fused_computation.19 | loop fusion | flops 8388608 | bytes 6300672 | tf_op jit(solution)/shard_map/convert_element_type | solution.py:113
  146.8 25.5 %slice.321 = bf16[4,2,4,64,256]{4,1,3,2,0:T(2,128)(2,1)} slice(bf16[4,4,4,64,256]{4,1,3,2,0:T(4,128)(2,1)S(1)} %fusion.4), slice={[0:4:1], [1:4:2], [0:4:1], [0:64:1], [0:256:1]} | slice | bytes 2097152 | tf_op jit(solution)/shard_map/slice | solution.py:118
  172.3 25.3 %slice.320 = bf16[4,2,4,64,256]{4,1,3,2,0:T(2,128)(2,1)} slice(bf16[4,4,4,64,256]{4,1,3,2,0:T(4,128)(2,1)S(1)} %fusion.4), slice={[0:4:1], [0:4:2], [0:4:1], [0:64:1], [0:256:1]} | slice | bytes 2097152 | tf_op jit(solution)/shard_map/slice | solution.py:118
  197.6 3.1 %multiply_convert_fusion = bf16[4,2,4,64,256]{4,1,3,2,0:T(2,128)(2,1)S(1)} fusion(bf16[4,2,4,64,256]{4,1,3,2,0:T(2,128)(2,1)} %slice.321, bf16[4,2,4,64,256]{4,1,3,2,0:T(2,128)(2,1)} %slice.320), kind=kLoop, calls=%fused_computation.44 | loop fusion | flops 2621440 | bytes 3145728 | tf_op jit(solution)/shard_map/convert_element_type | solution.py:119
  (125 shorter events, 35.9 us)
Async XLA Ops:
  0.0 202.4 %copy-start = (bf16[1024,256]{1,0:T(8,128)(2,1)S(1)}, bf16[1024,256]{1,0:T(8,128)(2,1)}, u32[]{:S(2)}) copy-start(bf16[1024,256]{1,0:T(8,128)(2,1)} %param.20) | copy-start | bytes 1572868
  4.8 20.5 %all-to-all-start = ((bf16[16,4,3,4,256]{4,3,2,1,0:T(4,128)(2,1)}), bf16[16,4,3,4,256]{4,3,2,1,0:T(4,128)(2,1)S(1)}, u32[]{:S(2)}, u32[]{:S(2)}) async-start(bf16[16,4,3,4,256]{4,3,2,1,0:T(4,128)(2,1)} %reshape.120), calls=%async_computation | async-start | bytes 786432 | tf_op jit(solution)/shard_map/all_to_all | solution.py:176
  25.5 17.2 %copy-start.11 = (bf16[81,128]{1,0:T(8,128)(2,1)S(1)}, bf16[81,128]{1,0:T(8,128)(2,1)}, u32[]{:S(2)}) copy-start(bf16[81,128]{1,0:T(8,128)(2,1)} %param.14) | copy-start | bytes 62212
  25.6 4.9 %collective-permute-start = (bf16[4,2,4,64,3]{3,2,4,1,0:T(4,128)(2,1)S(1)}, bf16[4,2,4,64,3]{3,2,4,1,0:T(4,128)(2,1)S(1)}, u32[]{:S(2)}, u32[]{:S(2)}) collective-permute-start(bf16[4,2,4,64,3]{3,2,4,1,0:T(4,128)(2,1)S(1)} %slice.325), channel_id=1, source_target_pairs={{0,1},{1,2},{2,3},{4,5},{5,6},{6,7},{8,9},{9,10},{10,11},{12,13},{... | collective-permute-start | bytes 36872 | tf_op jit(solution)/shard_map/ppermute | solution.py:14
  30.7 5.9 %collective-permute-start.2 = (bf16[4,6,1,64,3]{3,2,4,1,0:T(2,128)(2,1)S(1)}, bf16[4,6,1,64,3]{3,2,4,1,0:T(2,128)(2,1)S(1)}, u32[]{:S(2)}, u32[]{:S(2)}) collective-permute-start(bf16[4,6,1,64,3]{3,2,4,1,0:T(2,128)(2,1)S(1)} %get-tuple-element.48), channel_id=1, source_target_pairs={{4,0},{8,4},{12,8},{5,1},{9,5},{13,9},{6,2},{10,6},{14,10},{7,3},{... | collective-permute-start | bytes 27656 | tf_op jit(solution)/shard_map/ppermute | solution.py:27
  32.0 6.2 %collective-permute-start.1 = (bf16[4,6,1,64,3]{3,2,4,1,0:T(2,128)(2,1)S(1)}, bf16[4,6,1,64,3]{3,2,4,1,0:T(2,128)(2,1)S(1)}, u32[]{:S(2)}, u32[]{:S(2)}) collective-permute-start(bf16[4,6,1,64,3]{3,2,4,1,0:T(2,128)(2,1)S(1)} %get-tuple-element.47), channel_id=1, source_target_pairs={{0,4},{4,8},{8,12},{1,5},{5,9},{9,13},{2,6},{6,10},{10,14},{3,7},{... | collective-permute-start | bytes 27656 | tf_op jit(solution)/shard_map/ppermute | solution.py:25
  40.3 27.9 %copy-start.14 = (f32[128]{0:T(128)S(1)}, f32[128]{0:T(128)}, u32[]{:S(2)}) copy-start(f32[128]{0:T(128)} %param.15) | copy-start | bytes 1540
  40.3 27.9 %copy-start.15 = (f32[128]{0:T(128)S(1)}, f32[128]{0:T(128)}, u32[]{:S(2)}) copy-start(f32[128]{0:T(128)} %param.16) | copy-start | bytes 1540
  68.9 8.2 %collective-permute-start.3 = (bf16[4,2,4,64,128]{4,3,2,1,0:T(8,128)(2,1)S(1)}, bf16[4,2,4,64,128]{4,3,2,1,0:T(8,128)(2,1)S(1)}, u32[]{:S(2)}, u32[]{:S(2)}) collective-permute-start(bf16[4,2,4,64,128]{4,3,2,1,0:T(8,128)(2,1)S(1)} %slice.357), channel_id=1, source_target_pairs={{0,1},{1,2},{2,3},{4,5},{5,6},{6,7},{8,9},{9,10},{10,11},{12,13},{... | collective-permute-start | bytes 1572872 | tf_op jit(solution)/shard_map/ppermute | solution.py:14
  77.3 9.7 %collective-permute-start.5 = (bf16[4,6,1,64,128]{4,3,2,1,0:T(8,128)(2,1)S(1)}, bf16[4,6,1,64,128]{4,3,2,1,0:T(8,128)(2,1)S(1)}, u32[]{:S(2)}, u32[]{:S(2)}) collective-permute-start(bf16[4,6,1,64,128]{4,3,2,1,0:T(8,128)(2,1)S(1)} %get-tuple-element.44), channel_id=1, source_target_pairs={{4,0},{8,4},{12,8},{5,1},{9,5},{13,9},{6,2},{10,6},{14,10},{7,3},{... | collective-permute-start | bytes 1179656 | tf_op jit(solution)/shard_map/ppermute | solution.py:27
  78.6 9.8 %collective-permute-start.4 = (bf16[4,6,1,64,128]{4,3,2,1,0:T(8,128)(2,1)S(1)}, bf16[4,6,1,64,128]{4,3,2,1,0:T(8,128)(2,1)S(1)}, u32[]{:S(2)}, u32[]{:S(2)}) collective-permute-start(bf16[4,6,1,64,128]{4,3,2,1,0:T(8,128)(2,1)S(1)} %get-tuple-element.43), channel_id=1, source_target_pairs={{0,4},{4,8},{8,12},{1,5},{5,9},{9,13},{2,6},{6,10},{10,14},{3,7},{... | collective-permute-start | bytes 1179656 | tf_op jit(solution)/shard_map/ppermute | solution.py:25
  97.5 1.2 copy-start.1
  97.5 1.5 copy-start.2
  97.5 1.8 copy-start.3
  99.4 1.5 copy-start.8
  105.7 1.3 copy-start.6
  105.7 1.5 copy-start.7
  111.6 1.3 copy-start.4
  111.7 1.5 copy-start.5
  113.2 1.2 copy-start.9
  113.2 1.5 copy-start.10
  116.0 24.5 %copy-start.12 = (f32[256]{0:T(256)S(1)}, f32[256]{0:T(256)}, u32[]{:S(2)}) copy-start(f32[256]{0:T(256)} %param.18) | copy-start | bytes 3076
  116.0 24.6 %copy-start.13 = (f32[256]{0:T(256)S(1)}, f32[256]{0:T(256)}, u32[]{:S(2)}) copy-start(f32[256]{0:T(256)} %param.19) | copy-start | bytes 3076
  197.6 4.8 %copy-start.16 = (f32[256]{0:T(256)S(1)}, f32[256]{0:T(256)}, u32[]{:S(2)}) copy-start(f32[256]{0:T(256)} %param.21) | copy-start | bytes 3076
